TPU v7x, 128 devices: a whole 4x4x4 slice. The times are simulated.
128 devices in a mesh: blk: 32 (over x, z, y_hi), quarter: 4 (over y_lo, core).
Axes of the slice: x: 4, y: 4 (y_hi: 2, y_lo: 2; y = y_hi * 2 + y_lo), z: 4, core: 2. Of those that a mesh axis runs over, the one named last changes fastest.
Arguments:
- bints: bfloat16 [256, 512, 1280], P('blk', None, 'quarter'), may hold values from -2.5 to 2.5
- occ_energy: float32 [256], replicated, may hold values from -2 to -0.5
- vir_energy: float32 [512], replicated, may hold values from 0.2 to 3
Outputs:
- gamma: float32 [256, 512, 1280], P(('blk', 'quarter'))
- vvdens: float32 [512, 512], P(('blk', 'quarter'))
All inputs are finite; a program needn't handle non-finite values.
Results may differ from a plain program's by a relative error of at most 0.0016.
Values may be sent and summed in bfloat16 or wider, within the bound.
A program may use at most 128 MiB of HBM per device.

v0:
```python
import jax
import jax.numpy as jnp
from jax import lax
from jax.sharding import PartitionSpec as P

V = 512
CYCLE = 3


def shifted(shard, axis, by):
    devices = lax.axis_size(axis)
    return lax.ppermute(shard, axis, [(i, (i + by) % devices) for i in range(devices)])


def per_device(bints, occ_energy, vir_energy):
    local = lax.all_to_all(bints, "quarter", split_axis=0, concat_axis=2, tiled=True)
    quarters = lax.axis_size("quarter")
    block_count = lax.axis_size("blk")
    block_id = lax.axis_index("blk")
    quarter_id = lax.axis_index("quarter")
    occ_rows = local.shape[0]
    own_group = block_id * quarters + quarter_id
    own_energy = lax.dynamic_slice_in_dim(occ_energy, own_group * occ_rows, occ_rows)
    density = jnp.zeros(local.shape, jnp.float32)
    vv_part = jnp.zeros((V, V), jnp.float32)
    partner_block = local
    for step in range(CYCLE):
        if step > 0:
            partner_block = shifted(partner_block, "blk", 1)
        partner = (block_id - step) % block_count * quarters + quarter_id
        other_energy = lax.dynamic_slice_in_dim(occ_energy, partner * occ_rows, occ_rows)
        pairint = jnp.einsum(
            "iap,jbp->ijab", local, partner_block, preferred_element_type=jnp.float32
        )
        denom = (
            vir_energy[None, None, :, None]
            + vir_energy[None, None, None, :]
            - own_energy[:, None, None, None]
            - other_energy[None, :, None, None]
        )
        amp = pairint / denom
        amp_b = amp.astype(jnp.bfloat16)
        tilde = (2.0 * amp - jnp.swapaxes(amp, 2, 3)).astype(jnp.bfloat16)
        density = density + jnp.einsum(
            "ijab,jbp->iap", tilde, partner_block, preferred_element_type=jnp.float32
        )
        vv_part = vv_part + jnp.einsum(
            "ijac,ijbc->ab", amp_b, tilde, preferred_element_type=jnp.float32
        )
    row_count = V // (block_count * quarters)
    summed = lax.psum(vv_part, ("blk", "quarter"))
    rows_out = lax.dynamic_slice_in_dim(summed, own_group * row_count, row_count, 0)
    return (density, rows_out / PAIRS_SCALE(occ_rows, block_count, quarters))


def PAIRS_SCALE(occ_rows, block_count, quarters):
    return float(occ_rows * block_count * quarters * CYCLE * occ_rows)


def solution(mesh):
    return jax.shard_map(
        per_device,
        mesh=mesh,
        in_specs=(P("blk", None, "quarter"), P(), P()),
        out_specs=(P(("blk", "quarter"), None, None), P(("blk", "quarter"), None)),
        check_vma=False,
    )
```

profile of v0, /device:TPU:1, one launch (start us, length us, event | category | flops | bytes accessed | tf_op | source)
XLA Modules:
  0.0 359.4 jit_solution(8892862195207607736)
XLA Ops:
  7.2 0.0 all-reduce.2.cloned.1.call-start
  7.2 35.3 %all_to_all.18 = bf16[8,512,320]{1,2,0:T(8,128)(2,1)S(1)} all-to-all(bf16[8,512,320]{1,2,0:T(8,128)(2,1)} %param.3), channel_id=1, replica_groups=mesh['blk'=32,'quarter'=4] {'quarter'}, dimensions={0} | all-to-all | bytes 5242880 | tf_op jit(solution)/shard_map/all_to_all | solution.py:16
  42.5 0.0 copy-start
  42.5 0.2 copy.21
  42.6 1.3 copy-done
  44.0 0.0 copy-start.9
  44.0 0.0 copy-start.8
  44.0 2.6 copy.25
  46.5 3.0 collective-permute-start
  49.6 62.2 %collective-permute-done = bf16[2,512,1280]{2,1,0:T(8,128)(2,1)} collective-permute-done((bf16[2,512,1280]{2,1,0:T(8,128)(2,1)}, bf16[2,512,1280]{2,1,0:T(8,128)(2,1)}, u32[]{:S(2)}, u32[]{:S(2)}) %collective-permute-start) | collective-permute-done | bytes 2621472 | tf_op jit(solution)/shard_map/ppermute | solution.py:12
  111.7 0.0 collective-permute-start.1
  111.7 0.0 copy-done.9
  111.8 0.0 copy-start.1
  111.8 0.1 fusion.54
  111.8 0.0 copy-done.8
  111.8 0.1 broadcast_add_fusion
  112.0 1.7 broadcast_subtract_fusion
  113.6 0.3 copy-done.1
  113.9 4.5 %fusion.13 = f32[2,512,2,512,1]{3,1,4,2,0:T(8,128)} fusion(bf16[4,2,512,320]{2,3,1,0:T(8,128)(2,1)S(1)} %bitcast.95), kind=kOutput, calls=%fused_computation.21 | convolution fusion | flops 2684354560 | bytes 6815744 | tf_op jit(solution)/shard_map/iap,jbp->ijab/dot_general | solution.py:32
  118.4 5.2 %copy.22 = f32[2,512,2,512]{1,3,2,0:T(8,128)} copy(f32[2,512,2,512]{3,1,2,0:T(8,128)} %bitcast.89) | data formatting | bytes 8388608 | tf_op jit(solution)/shard_map/iap,jbp->ijab/dot_general | solution.py:32
  123.6 6.2 %fusion.11 = f32[2,512,2,512]{3,1,2,0:T(8,128)} fusion(bf16[2,512,1280,1]{1,2,0,3:T(8,128)(2,1)S(1)} %bitcast.91, bf16[2,512,1280]{2,1,0:T(8,128)(2,1)} %collective-permute-done), kind=kOutput, calls=%fused_computation.19 | convolution fusion | flops 2684354560 | bytes 9437184 | tf_op jit(solution)/shard_map/iap,jbp->ijab/dot_general | solution.py:32
  129.8 5.3 %copy.27 = f32[2,512,2,512]{1,3,2,0:T(8,128)} copy(f32[2,512,2,512]{3,1,2,0:T(8,128)} %fusion.11) | data formatting | bytes 8388608 | tf_op jit(solution)/shard_map/iap,jbp->ijab/dot_general | solution.py:32
  135.1 39.5 %collective-permute-done.1 = bf16[2,512,1280]{2,1,0:T(8,128)(2,1)} collective-permute-done((bf16[2,512,1280]{2,1,0:T(8,128)(2,1)}, bf16[2,512,1280]{2,1,0:T(8,128)(2,1)}, u32[]{:S(2)}, u32[]{:S(2)}) %collective-permute-start.1) | collective-permute-done | bytes 2621472 | tf_op jit(solution)/shard_map/ppermute | solution.py:12
  174.6 6.1 %fusion.7 = f32[2,512,2,512]{3,1,2,0:T(8,128)} fusion(bf16[2,512,1280,1]{1,2,0,3:T(8,128)(2,1)S(1)} %bitcast.92, bf16[2,512,1280]{2,1,0:T(8,128)(2,1)} %collective-permute-done.1), kind=kOutput, calls=%fused_computation.15 | convolution fusion | flops 2684354560 | bytes 9437184 | tf_op jit(solution)/shard_map/iap,jbp->ijab/dot_general | solution.py:32
  180.7 5.2 %copy.30 = f32[2,512,2,512]{1,3,2,0:T(8,128)} copy(f32[2,512,2,512]{3,1,2,0:T(8,128)} %fusion.7) | data formatting | bytes 8388608 | tf_op jit(solution)/shard_map/iap,jbp->ijab/dot_general | solution.py:32
  185.9 12.9 %fusion.52 = (bf16[2,2,512,512]{3,2,0,1:T(8,128)(2,1)S(1)}, bf16[2,2,512,512]{3,2,0,1:T(8,128)(2,1)S(1)}, bf16[2,2,512,512]{3,2,0,1:T(8,128)(2,1)S(1)}, bf16[2,2...) fusion(f32[2]{0:T(128)S(1)} %get-tuple-element.12, ...), kind=kLoop, calls=%fused_computation.42 | loop fusion | flops 22020096 | bytes 39845912 | tf_op jit(solution)/shard_map/convert_element_type | solution.py:42
  198.8 0.0 copy-start.6
  198.8 0.0 copy-start.4
  198.8 0.0 copy-start.2
  198.9 0.0 copy-start.7
  198.9 4.6 %fusion.25 = f32[512,512]{1,0:T(8,128)S(1)} fusion(bf16[2,2,512,512]{3,2,0,1:T(8,128)(2,1)S(1)} %get-tuple-element.10, bf16[2,2,512,512]{3,2,0,1:T(8,128)(2,1)} %get-tuple-element.11), kind=kOutput, calls=%fused_computation.33 | convolution fusion | flops 1073741824 | bytes 5242880 | tf_op jit(solution)/shard_map/ijac,ijbc->ab/dot_general | solution.py:47
  203.4 0.0 copy-done.6
  203.5 0.0 copy-done.4
  203.5 0.0 copy-done.7
  203.5 1.3 fusion.45
  204.8 0.0 copy-done.2
  204.8 2.3 fusion.40
  207.1 0.0 all-reduce.2.cloned.1.call-update
  207.1 0.0 copy-start.5
  207.1 4.6 %fusion.55 = f32[2,512,1280,1]{2,1,0,3:T(8,128)S(1)} fusion(bf16[2,2,512,512]{3,2,0,1:T(8,128)(2,1)} %copy-done.6, bf16[2,512,1280,1]{1,2,3,0:T(8,128)(2,1)S(1)} %bitcast.93), kind=kOutput, calls=%fused_computation.46 | convolution fusion | flops 2684354560 | bytes 9961472 | tf_op jit(solution)/shard_map/ijab,jbp->iap/dot_general | solution.py:44
  211.7 0.0 copy-done.5
  211.7 0.0 copy-start.3
  211.8 4.8 %fusion.9 = f32[2,512,1280,1]{2,1,0,3:T(8,128)S(1)} fusion(bf16[2,2,512,512]{3,2,0,1:T(8,128)(2,1)S(1)} %copy-done.5, bf16[2,512,1280]{2,1,0:T(8,128)(2,1)} %collective-permute-done), kind=kOutput, calls=%fused_computation.17 | convolution fusion | flops 2684354560 | bytes 9961472 | tf_op jit(solution)/shard_map/ijab,jbp->iap/dot_general | solution.py:44
  216.5 0.0 copy-done.3
  216.5 6.3 %bitcast_add_fusion = f32[2,512,1280]{2,1,0:T(8,128)} fusion(f32[2,512,1280,1]{2,1,0,3:T(8,128)S(1)} %fusion.9, f32[2,512,1280,1]{2,1,0,3:T(8,128)S(1)} %fusion.55, bf16[2,2,512,512]{3,2,0,1:T(8,128)(2,1)S(1)} %copy-done.3, bf16[2,512,1280]{2,1,0:T(8,128)(2,1)} %collective-permute-done.1), kind=kOutput, calls=%fused_computation.6 | convolution fusion | flops 2686976000 | bytes 20447232 | tf_op jit(solution)/shard_map/ijab,jbp->iap/dot_general | solution.py:44
  222.9 128.3 %all-reduce.2.cloned.1.call-done = f32[512,512]{1,0:T(8,128)} async-done(((f32[512,512]{1,0:T(8,128)}), f32[512,512]{1,0:T(8,128)}) %all-reduce.2.cloned.1.call-update) | async-done | bytes 1048592 | tf_op jit(solution)/shard_map/psum | solution.py:51
  351.2 1.3 dynamic-slice_multiply_fusion
Async XLA Ops:
  7.2 344.1 %all-reduce.2.cloned.1.call-start = ((), (), s32[]{:S(2)}) async-start(), calls=%async_computation.1 | async-start | bytes 2097152 | tf_op jit(solution)/shard_map/psum | solution.py:51
  42.5 1.5 copy-start
  44.0 67.8 %copy-start.9 = (f32[256]{0:T(256)S(1)}, f32[256]{0:T(256)}, u32[]{:S(2)}) copy-start(f32[256]{0:T(256)} %param.4) | copy-start | bytes 3076
  44.0 67.9 %copy-start.8 = (f32[512]{0:T(512)S(1)}, f32[512]{0:T(512)}, u32[]{:S(2)}) copy-start(f32[512]{0:T(512)} %param.5) | copy-start | bytes 6148
  46.5 65.2 %collective-permute-start = (bf16[2,512,1280]{2,1,0:T(8,128)(2,1)}, bf16[2,512,1280]{2,1,0:T(8,128)(2,1)}, u32[]{:S(2)}, u32[]{:S(2)}) collective-permute-start(bf16[2,512,1280]{2,1,0:T(8,128)(2,1)} %copy.25), channel_id=1, source_target_pairs={{0,4},{4,8},{8,12},{12,16},{16,20},{20,24},{24,28},{28,32},{32,36}... | collective-permute-start | bytes 7864328 | tf_op jit(solution)/shard_map/ppermute | solution.py:12
  111.7 62.8 %collective-permute-start.1 = (bf16[2,512,1280]{2,1,0:T(8,128)(2,1)}, bf16[2,512,1280]{2,1,0:T(8,128)(2,1)}, u32[]{:S(2)}, u32[]{:S(2)}) collective-permute-start(bf16[2,512,1280]{2,1,0:T(8,128)(2,1)} %collective-permute-done), channel_id=1, source_target_pairs={{0,4},{4,8},{8,12},{12,16},{16,20},{20,24},{24,28},{28,32},{32,36}... | collective-permute-start | bytes 7864328 | tf_op jit(solution)/shard_map/ppermute | solution.py:12
  111.8 2.2 copy-start.1
  198.8 4.6 %copy-start.6 = (bf16[2,2,512,512]{3,2,0,1:T(8,128)(2,1)}, bf16[2,2,512,512]{3,2,0,1:T(8,128)(2,1)S(1)}, u32[]{:S(2)}) copy-start(bf16[2,2,512,512]{3,2,0,1:T(8,128)(2,1)S(1)} %get-tuple-element.10) | copy-start | bytes 6291460
  198.8 4.6 %copy-start.4 = (bf16[2,2,512,512]{3,2,0,1:T(8,128)(2,1)}, bf16[2,2,512,512]{3,2,0,1:T(8,128)(2,1)S(1)}, u32[]{:S(2)}) copy-start(bf16[2,2,512,512]{3,2,0,1:T(8,128)(2,1)S(1)} %get-tuple-element.8) | copy-start | bytes 6291460
  198.8 5.9 %copy-start.2 = (bf16[2,2,512,512]{3,2,0,1:T(8,128)(2,1)}, bf16[2,2,512,512]{3,2,0,1:T(8,128)(2,1)S(1)}, u32[]{:S(2)}) copy-start(bf16[2,2,512,512]{3,2,0,1:T(8,128)(2,1)S(1)} %get-tuple-element.3) | copy-start | bytes 6291460
  198.9 4.6 %copy-start.7 = (bf16[2,2,512,512]{3,2,0,1:T(8,128)(2,1)S(1)}, bf16[2,2,512,512]{3,2,0,1:T(8,128)(2,1)}, u32[]{:S(2)}) copy-start(bf16[2,2,512,512]{3,2,0,1:T(8,128)(2,1)} %get-tuple-element.9) | copy-start | bytes 6291460
  207.1 4.7 %copy-start.5 = (bf16[2,2,512,512]{3,2,0,1:T(8,128)(2,1)S(1)}, bf16[2,2,512,512]{3,2,0,1:T(8,128)(2,1)}, u32[]{:S(2)}) copy-start(bf16[2,2,512,512]{3,2,0,1:T(8,128)(2,1)} %copy-done.4) | copy-start | bytes 6291460
  211.7 4.8 %copy-start.3 = (bf16[2,2,512,512]{3,2,0,1:T(8,128)(2,1)S(1)}, bf16[2,2,512,512]{3,2,0,1:T(8,128)(2,1)}, u32[]{:S(2)}) copy-start(bf16[2,2,512,512]{3,2,0,1:T(8,128)(2,1)} %copy-done.2) | copy-start | bytes 6291460
Sparse Core Ops, SparseCore 0:
  207.2 143.9 all-reduce.1
where the time goes:
time: 360 us; the launch traced here: 359 us
  waiting for transfers between devices  230 us (64%)
  matrix products  40.6 us (11%)
  blocking collectives  35.3 us (10%)
  local copies, waits for them, and re-layouts  20.2 us (6%)
  other arithmetic  16 us (4%)
  between operations  14.2 us (4%)
    psum x1, waiting for transfers between devices, per_device(): summed = lax.psum(vv_part, ('blk', 'quarter'))  128 us
    ppermute x2, waiting for transfers between devices, shifted(): lax.ppermute(shard, axis, [(i, (i + by) % devices) for i in range(devices)])  102 us
    all_to_all x1, blocking collectives, per_device(): lax.all_to_all(bints, 'quarter', split_axis=0, concat_axis=2, tiled=True)  35.3 us
    dot_general x3, matrix products, per_device(): jnp.einsum('iap,jbp->ijab', local, partner_block, preferred_element_type=...  16.8 us
    dot_general x3, local copies, waits for them, and re-layouts, per_device(): jnp.einsum('iap,jbp->ijab', local, partner_block, preferred_element_type=...  15.8 us
    dot_general x3, matrix products, per_device(): jnp.einsum('ijab,jbp->iap', tilde, partner_block, preferred_element_type=...  15.7 us
    convert_element_type x1, other arithmetic, per_device(): amp_b = amp.astype(jnp.bfloat16)  12.9 us
    dot_general x3, matrix products, per_device(): jnp.einsum('ijac,ijbc->ab', amp_b, tilde, preferred_element_type=jnp.floa...  8.13 us
  transfers between devices with their start and end apart: 3, of which 3 were waited for; matrix products, arithmetic and copies ran while one was open for 11% of the time, Pallas kernels for 0%

commit v1 on v0

--- a/solution.py
+++ b/solution.py
@@ -48,7 +48,7 @@
             "ijac,ijbc->ab", amp_b, tilde, preferred_element_type=jnp.float32
         )
     row_count = V // (block_count * quarters)
-    summed = lax.psum(vv_part, ("blk", "quarter"))
+    summed = lax.psum(lax.psum(vv_part, "quarter"), "blk")
     rows_out = lax.dynamic_slice_in_dim(summed, own_group * row_count, row_count, 0)
     return (density, rows_out / PAIRS_SCALE(occ_rows, block_count, quarters))
 

time: 360 us -> 610 us (1.69)
  the two profiles are of different devices: /device:TPU:1 before, /device:TPU:0 now
where the time goes in v1:
time: 610 us; the launch traced here: 609 us
  waiting for transfers between devices  474 us (78%)
  matrix products  46.2 us (8%)
  blocking collectives  34.9 us (6%)
  local copies, waits for them, and re-layouts  20.2 us (3%)
  other arithmetic  16 us (3%)
  between operations  14.1 us (2%)
    psum x2, waiting for transfers between devices, per_device(): summed = lax.psum(lax.psum(vv_part, 'quarter'), 'blk')  371 us
    ppermute x2, waiting for transfers between devices, shifted(): lax.ppermute(shard, axis, [(i, (i + by) % devices) for i in range(devices)])  103 us
    all_to_all x1, blocking collectives, per_device(): lax.all_to_all(bints, 'quarter', split_axis=0, concat_axis=2, tiled=True)  34.9 us
    dot_general x3, matrix products, per_device(): jnp.einsum('ijab,jbp->iap', tilde, partner_block, preferred_element_type=...  21.3 us
    dot_general x3, matrix products, per_device(): jnp.einsum('iap,jbp->ijab', local, partner_block, preferred_element_type=...  16.8 us
    dot_general x3, local copies, waits for them, and re-layouts, per_device(): jnp.einsum('iap,jbp->ijab', local, partner_block, preferred_element_type=...  15.8 us
    convert_element_type x1, other arithmetic, per_device(): amp_b = amp.astype(jnp.bfloat16)  12.9 us
  transfers between devices with their start and end apart: 4, of which 4 were waited for; matrix products, arithmetic and copies ran while one was open for 7% of the time, Pallas kernels for 0%

profile of v1, /device:TPU:0, one launch (start us, length us, event | category | flops | bytes accessed | tf_op | source)
XLA Modules:
  0.0 609.4 jit_solution(6891630874351233915)
XLA Ops:
  7.2 0.0 all-reduce.3.cloned.1.call-start
  7.2 34.9 %all_to_all.18 = bf16[8,512,320]{1,2,0:T(8,128)(2,1)S(1)} all-to-all(bf16[8,512,320]{1,2,0:T(8,128)(2,1)} %param.3), channel_id=1, replica_groups=mesh['blk'=32,'quarter'=4] {'quarter'}, dimensions={0} | all-to-all | bytes 5242880 | tf_op jit(solution)/shard_map/all_to_all | solution.py:16
  42.1 0.0 copy-start
  42.1 0.2 copy.21
  42.3 1.3 copy-done
  43.6 0.0 copy-start.9
  43.6 0.0 copy-start.8
  43.6 2.6 copy.25
  46.2 3.3 collective-permute-start
  49.5 62.5 %collective-permute-done = bf16[2,512,1280]{2,1,0:T(8,128)(2,1)} collective-permute-done((bf16[2,512,1280]{2,1,0:T(8,128)(2,1)}, bf16[2,512,1280]{2,1,0:T(8,128)(2,1)}, u32[]{:S(2)}, u32[]{:S(2)}) %collective-permute-start) | collective-permute-done | bytes 2621472 | tf_op jit(solution)/shard_map/ppermute | solution.py:12
  112.0 0.0 collective-permute-start.1
  112.0 0.0 copy-done.9
  112.0 0.0 copy-start.1
  112.0 0.1 fusion.54
  112.1 0.0 copy-done.8
  112.1 0.1 broadcast_add_fusion
  112.2 1.7 broadcast_subtract_fusion
  113.9 0.3 copy-done.1
  114.2 4.5 fusion.13
  118.6 5.2 copy.22
  123.9 6.2 %fusion.11 = f32[2,512,2,512]{3,1,2,0:T(8,128)} fusion(bf16[2,512,1280,1]{1,2,0,3:T(8,128)(2,1)S(1)} %bitcast.91, bf16[2,512,1280]{2,1,0:T(8,128)(2,1)} %collective-permute-done), kind=kOutput, calls=%fused_computation.19 | convolution fusion | flops 2684354560 | bytes 9437184 | tf_op jit(solution)/shard_map/iap,jbp->ijab/dot_general | solution.py:32
  130.1 5.3 copy.27
  135.3 40.3 %collective-permute-done.1 = bf16[2,512,1280]{2,1,0:T(8,128)(2,1)} collective-permute-done((bf16[2,512,1280]{2,1,0:T(8,128)(2,1)}, bf16[2,512,1280]{2,1,0:T(8,128)(2,1)}, u32[]{:S(2)}, u32[]{:S(2)}) %collective-permute-start.1) | collective-permute-done | bytes 2621472 | tf_op jit(solution)/shard_map/ppermute | solution.py:12
  175.7 6.1 %fusion.7 = f32[2,512,2,512]{3,1,2,0:T(8,128)} fusion(bf16[2,512,1280,1]{1,2,0,3:T(8,128)(2,1)S(1)} %bitcast.92, bf16[2,512,1280]{2,1,0:T(8,128)(2,1)} %collective-permute-done.1), kind=kOutput, calls=%fused_computation.15 | convolution fusion | flops 2684354560 | bytes 9437184 | tf_op jit(solution)/shard_map/iap,jbp->ijab/dot_general | solution.py:32
  181.8 5.2 copy.30
  187.0 12.9 %fusion.52 = (bf16[2,2,512,512]{3,2,0,1:T(8,128)(2,1)S(1)}, bf16[2,2,512,512]{3,2,0,1:T(8,128)(2,1)S(1)}, bf16[2,2,512,512]{3,2,0,1:T(8,128)(2,1)S(1)}, bf16[2,2...) fusion(f32[2]{0:T(128)S(1)} %get-tuple-element.12, ...), kind=kLoop, calls=%fused_computation.42 | loop fusion | flops 22020096 | bytes 39845912 | tf_op jit(solution)/shard_map/convert_element_type | solution.py:42
  199.9 0.0 copy-start.6
  199.9 0.0 copy-start.2
  200.0 0.0 copy-start.7
  200.0 4.6 fusion.25
  204.5 0.0 copy-done.6
  204.5 0.0 copy-done.4
  204.6 0.0 copy-done.7
  204.6 1.3 fusion.45
  205.8 0.0 copy-done.2
  205.9 2.3 fusion.40
  208.1 0.0 all-reduce.3.cloned.1.call-update
  208.1 0.2 all-reduce.5.cloned.1.call-start
  208.4 0.0 copy-start.5
  208.4 7.0 %fusion.55 = f32[2,512,1280,1]{2,1,0,3:T(8,128)} fusion(bf16[2,2,512,512]{3,2,0,1:T(8,128)(2,1)} %copy-done.6, bf16[2,512,1280,1]{1,2,3,0:T(8,128)(2,1)S(1)} %bitcast.93), kind=kOutput, calls=%fused_computation.46 | convolution fusion | flops 2684354560 | bytes 9961472 | tf_op jit(solution)/shard_map/ijab,jbp->iap/dot_general | solution.py:44
  215.3 0.0 copy-done.5
  215.4 6.5 %fusion.9 = f32[2,512,1280,1]{2,1,0,3:T(8,128)} fusion(bf16[2,2,512,512]{3,2,0,1:T(8,128)(2,1)S(1)} %copy-done.5, bf16[2,512,1280]{2,1,0:T(8,128)(2,1)} %collective-permute-done), kind=kOutput, calls=%fused_computation.17 | convolution fusion | flops 2684354560 | bytes 9961472 | tf_op jit(solution)/shard_map/ijab,jbp->iap/dot_general | solution.py:44
  221.8 21.5 %all-reduce.3.cloned.1.call-done = f32[512,512]{1,0:T(8,128)} async-done(((f32[512,512]{1,0:T(8,128)}), f32[512,512]{1,0:T(8,128)}) %all-reduce.3.cloned.1.call-update) | async-done | bytes 1048592 | tf_op jit(solution)/shard_map/psum | solution.py:51
  243.4 0.0 all-reduce.5.cloned.1.call-update
  243.4 0.0 copy-done.3
  243.4 7.9 %bitcast_add_fusion = f32[2,512,1280]{2,1,0:T(8,128)} fusion(f32[2,512,1280,1]{2,1,0,3:T(8,128)} %fusion.9, f32[2,512,1280,1]{2,1,0,3:T(8,128)} %fusion.55, bf16[2,2,512,512]{3,2,0,1:T(8,128)(2,1)S(1)} %copy-done.3, bf16[2,512,1280]{2,1,0:T(8,128)(2,1)} %collective-permute-done.1), kind=kOutput, calls=%fused_computation.6 | convolution fusion | flops 2686976000 | bytes 20447232 | tf_op jit(solution)/shard_map/ijab,jbp->iap/dot_general | solution.py:44
  251.3 349.9 %all-reduce.5.cloned.1.call-done = f32[512,512]{1,0:T(8,128)} async-done(((f32[512,512]{1,0:T(8,128)}), f32[512,512]{1,0:T(8,128)}) %all-reduce.5.cloned.1.call-update) | async-done | bytes 1048592 | tf_op jit(solution)/shard_map/psum | solution.py:51
  601.2 1.3 dynamic-slice_multiply_fusion
  (2 shorter events, 0.0 us)
Async XLA Ops:
  7.2 236.2 %all-reduce.3.cloned.1.call-start = ((), (), s32[]{:S(2)}) async-start(), calls=%async_computation.1 | async-start | bytes 2097152 | tf_op jit(solution)/shard_map/psum | solution.py:51
  42.1 1.5 copy-start
  43.6 68.4 %copy-start.9 = (f32[256]{0:T(256)S(1)}, f32[256]{0:T(256)}, u32[]{:S(2)}) copy-start(f32[256]{0:T(256)} %param.4) | copy-start | bytes 3076
  43.6 68.4 %copy-start.8 = (f32[512]{0:T(512)S(1)}, f32[512]{0:T(512)}, u32[]{:S(2)}) copy-start(f32[512]{0:T(512)} %param.5) | copy-start | bytes 6148
  46.2 65.8 %collective-permute-start = (bf16[2,512,1280]{2,1,0:T(8,128)(2,1)}, bf16[2,512,1280]{2,1,0:T(8,128)(2,1)}, u32[]{:S(2)}, u32[]{:S(2)}) collective-permute-start(bf16[2,512,1280]{2,1,0:T(8,128)(2,1)} %copy.25), channel_id=1, source_target_pairs={{0,4},{4,8},{8,12},{12,16},{16,20},{20,24},{24,28},{28,32},{32,36}... | collective-permute-start | bytes 7864328 | tf_op jit(solution)/shard_map/ppermute | solution.py:12
  112.0 63.7 %collective-permute-start.1 = (bf16[2,512,1280]{2,1,0:T(8,128)(2,1)}, bf16[2,512,1280]{2,1,0:T(8,128)(2,1)}, u32[]{:S(2)}, u32[]{:S(2)}) collective-permute-start(bf16[2,512,1280]{2,1,0:T(8,128)(2,1)} %collective-permute-done), channel_id=1, source_target_pairs={{0,4},{4,8},{8,12},{12,16},{16,20},{20,24},{24,28},{28,32},{32,36}... | collective-permute-start | bytes 7864328 | tf_op jit(solution)/shard_map/ppermute | solution.py:12
  112.0 2.2 copy-start.1
  199.9 4.6 copy-start.6
  199.9 4.6 copy-start.4
  199.9 5.9 copy-start.2
  200.0 4.6 copy-start.7
  208.1 393.1 %all-reduce.5.cloned.1.call-start = ((), (), s32[]{:S(2)}) async-start(), calls=%async_computation.2 | async-start | bytes 2097152 | tf_op jit(solution)/shard_map/psum | solution.py:51
  208.4 7.0 %copy-start.5 = (bf16[2,2,512,512]{3,2,0,1:T(8,128)(2,1)S(1)}, bf16[2,2,512,512]{3,2,0,1:T(8,128)(2,1)}, u32[]{:S(2)}) copy-start(bf16[2,2,512,512]{3,2,0,1:T(8,128)(2,1)} %copy-done.4) | copy-start | bytes 6291460
  215.3 28.0 %copy-start.3 = (bf16[2,2,512,512]{3,2,0,1:T(8,128)(2,1)S(1)}, bf16[2,2,512,512]{3,2,0,1:T(8,128)(2,1)}, u32[]{:S(2)}) copy-start(bf16[2,2,512,512]{3,2,0,1:T(8,128)(2,1)} %copy-done.2) | copy-start | bytes 6291460
Sparse Core Ops, SparseCore 0:
  208.3 35.0 all-reduce.2
  245.8 355.3 all-reduce.4
